TPU v7x, 32 devices: a whole 2x2x4 slice. The times are simulated.
32 devices in a mesh: cell: 8 (over z, x), desc: 4 (over y, core).
Axes of the slice: x: 2, y: 2, z: 4, core: 2. Of those that a mesh axis runs over, the one named last changes fastest.
Arguments:
- cells: float32 [8192, 256], P('cell'), may hold values from -128 to 128
- descs: float32 [8192, 256], P('desc'), may hold values from -4 to 4
- g_start: float32 [8192], P('desc'), may hold values from -8 to 8
- cot_f: float32 [8192], P('cell'), may hold values from -24 to 24
- cot_g: float32 [8192], P('desc'), may hold values from -24 to 24
Outputs:
- grad_cells: float32 [8192, 256], P('cell')
- grad_descs: float32 [8192, 256], P('desc')
All inputs are finite; a program needn't handle non-finite values.
Results may differ from a plain program's by a relative error of at most 0.0003.
Values sent between devices are 32-bit elements; how exact they have to be, the bound alone decides.
A program may use at most 192 MiB of HBM per device.

v0:
```python
import functools
import math

import jax
import jax.numpy as jnp
from jax import lax
from jax.experimental import pallas as pl
from jax.experimental.pallas import tpu as pltpu
from jax.sharding import PartitionSpec as P

ITERS = 4
MESH = pl.DeviceIdType.MESH
LANES = 128
F32 = jnp.float32
BF16 = jnp.bfloat16


def tree(op, parts):
    parts = list(parts)
    while len(parts) > 1:
        parts = [op(parts[i], parts[i + 1]) if i + 1 < len(parts) else parts[i] for i in range(0, len(parts), 2)]
    return parts[0]


def rotate(start, offset, count):
    return lax.rem(start + offset + count, count)


def send_all(axis, count, me, buf, send_sem, recv_sem, index):
    for off in range(1, count):
        peer = rotate(me, off, count)
        pltpu.make_async_remote_copy(
            src_ref=buf.at[index, me],
            dst_ref=buf.at[index, me],
            send_sem=send_sem.at[index, off],
            recv_sem=recv_sem.at[index, me],
            device_id={axis: peer},
            device_id_type=MESH,
        ).start()


def wait_all(axis, count, me, buf, send_sem, recv_sem, index):
    for off in range(1, count):
        source = rotate(me, -off, count)
        peer = rotate(me, off, count)
        got = pltpu.make_async_remote_copy(
            src_ref=buf.at[index, source],
            dst_ref=buf.at[index, source],
            send_sem=send_sem.at[index, off],
            recv_sem=recv_sem.at[index, source],
            device_id={axis: peer},
            device_id_type=MESH,
        )
        got.wait_recv()
        got.wait_send()


def split(value):
    high = value.astype(BF16)
    return high, (value - high.astype(F32)).astype(BF16)


def dot3(a_high, a_low, b_high, b_low):
    dot = functools.partial(jnp.dot, preferred_element_type=F32)
    return dot(a_high, b_high) + (dot(a_low, b_high) + dot(a_high, b_low))


def plan_kernel(
    n_cell, n_desc,
    cells, descs, g_first, cf, cg,
    px, py,
    logit, bplan, lbar, vcol, racc_m, racc_s, cacc_m, cacc_s, wide_a, wide_b,
    f_all, g_all, gbar, d_high, d_low, c_high, c_low,
    row_buf, col_buf, fbar_buf, gbar_buf,
    row_send, row_recv, col_send, col_recv, fb_send, fb_recv, gb_send, gb_recv,
    part_x, got_x, part_y, got_y, x_send, x_recv, y_send, y_recv,
):
    rows, width = cells.shape
    cols = descs.shape[0]
    scale = 2.0 / math.sqrt(width)
    my_cell = lax.axis_index("cell")
    my_desc = lax.axis_index("desc")
    blocks = cols // LANES
    x_block = rows // n_desc
    y_block = cols // n_cell
    group = 16
    unroll = 4

    barrier = pltpu.get_barrier_semaphore()
    for off in range(1, n_desc):
        pl.semaphore_signal(barrier, inc=1, device_id={"desc": rotate(my_desc, off, n_desc)}, device_id_type=MESH)
    for off in range(1, n_cell):
        pl.semaphore_signal(barrier, inc=1, device_id={"cell": rotate(my_cell, off, n_cell)}, device_id_type=MESH)

    def multiply(i, _):
        at = pl.ds(pl.multiple_of(i * 256, 256), 256)
        logit[at, :] = scale * lax.dot_general(
            cells[at, :], descs[...], (((1,), (1,)), ((), ())),
            precision=lax.Precision.HIGHEST, preferred_element_type=F32,
        )
        return 0

    lax.fori_loop(0, rows // 256, multiply, 0)
    g_all[0] = g_first[...]
    gbar[...] = cg[...]
    pl.semaphore_wait(barrier, n_desc + n_cell - 2)

    def spread_rows(vector):
        vcol[...] = jnp.broadcast_to(vector, (LANES, rows)).T

    def lane(b):
        return slice(b * LANES, (b + 1) * LANES)

    def forward(k, _):
        wide_a[...] = jnp.broadcast_to(g_all[k], (8, cols))

        def row_pass(i, _):
            for u in range(unroll):
                at = pl.ds(pl.multiple_of((i * unroll + u) * 8, 8), 8)
                parts = [logit[at, lane(b)] + wide_a[:, lane(b)] for b in range(blocks)]
                top = tree(jnp.maximum, parts)
                racc_m[at, :] = top
                racc_s[at, :] = tree(jnp.add, [jnp.exp(part - top) for part in parts])
            return 0

        lax.fori_loop(0, rows // (8 * unroll), row_pass, 0)
        tops = racc_m[...].T
        top = jnp.max(tops, axis=0, keepdims=True)
        row_buf[k, my_desc, 0:1, :] = top
        row_buf[k, my_desc, 1:2, :] = jnp.sum(racc_s[...].T * jnp.exp(tops - top), axis=0, keepdims=True)
        send_all("desc", n_desc, my_desc, row_buf, row_send, row_recv, k)
        wait_all("desc", n_desc, my_desc, row_buf, row_send, row_recv, k)
        tops = [row_buf[k, p, 0:1, :] for p in range(n_desc)]
        top = tree(jnp.maximum, tops)
        total = tree(jnp.add, [row_buf[k, p, 1:2, :] * jnp.exp(tops[p] - top) for p in range(n_desc)])
        f_now = -(top + jnp.log(total))
        f_all[k] = f_now
        spread_rows(f_now)
        cacc_m[...] = jnp.full((8, cols), -jnp.inf, F32)
        cacc_s[...] = jnp.zeros((8, cols), F32)

        def col_pass(i, _):
            base = i * (8 * group)
            for b in range(blocks):
                ats = [pl.ds(pl.multiple_of(base + 8 * u, 8), 8) for u in range(group)]
                parts = [logit[at, lane(b)] + vcol[at, :] for at in ats]
                before = cacc_m[:, lane(b)]
                top = jnp.maximum(before, tree(jnp.maximum, parts))
                cacc_m[:, lane(b)] = top
                cacc_s[:, lane(b)] = cacc_s[:, lane(b)] * jnp.exp(before - top) + tree(
                    jnp.add, [jnp.exp(part - top) for part in parts]
                )
            return 0

        lax.fori_loop(0, rows // (8 * group), col_pass, 0)
        top = jnp.max(cacc_m[...], axis=0, keepdims=True)
        col_buf[k, my_cell, 0:1, :] = top
        col_buf[k, my_cell, 1:2, :] = jnp.sum(cacc_s[...] * jnp.exp(cacc_m[...] - top), axis=0, keepdims=True)
        send_all("cell", n_cell, my_cell, col_buf, col_send, col_recv, k)
        wait_all("cell", n_cell, my_cell, col_buf, col_send, col_recv, k)
        tops = [col_buf[k, p, 0:1, :] for p in range(n_cell)]
        top = tree(jnp.maximum, tops)
        total = tree(jnp.add, [col_buf[k, p, 1:2, :] * jnp.exp(tops[p] - top) for p in range(n_cell)])
        g_all[k + 1] = -(top + jnp.log(total))
        return 0

    lax.fori_loop(0, ITERS, forward, 0)

    def backward(t, _):
        k = ITERS - 1 - t
        wide_a[...] = jnp.broadcast_to(g_all[k + 1], (8, cols))
        wide_b[...] = jnp.broadcast_to(gbar[...], (8, cols))
        spread_rows(f_all[k])

        def row_pass(i, _):
            for u in range(unroll):
                at = pl.ds(pl.multiple_of((i * unroll + u) * 8, 8), 8)
                f_here = vcol[at, :]
                terms = []
                for b in range(blocks):
                    value = jnp.exp((logit[at, lane(b)] + f_here) + wide_a[:, lane(b)])
                    bplan[at, lane(b)] = value
                    terms.append(value * wide_b[:, lane(b)])
                racc_s[at, :] = tree(jnp.add, terms)
            return 0

        lax.fori_loop(0, rows // (8 * unroll), row_pass, 0)
        fbar_buf[k, my_desc] = jnp.sum(racc_s[...].T, axis=0, keepdims=True)
        send_all("desc", n_desc, my_desc, fbar_buf, fb_send, fb_recv, k)
        wait_all("desc", n_desc, my_desc, fbar_buf, fb_send, fb_recv, k)
        fbar = -tree(jnp.add, [fbar_buf[k, p] for p in range(n_desc)])
        fbar = fbar + jnp.where(t == 0, cf[...], 0.0)
        spread_rows(fbar)
        ratio = jnp.exp(g_all[k] - g_all[k + 1])
        wide_a[...] = jnp.broadcast_to(ratio, (8, cols))
        cacc_s[...] = jnp.zeros((8, cols), F32)

        def col_pass(first):
            def body(i, _):
                base = i * (8 * group)
                for b in range(blocks):
                    terms = []
                    for u in range(group):
                        at = pl.ds(pl.multiple_of(base + 8 * u, 8), 8)
                        value = bplan[at, lane(b)]
                        term = value * vcol[at, :]
                        terms.append(term)
                        update = value * wide_b[:, lane(b)] + term * wide_a[:, lane(b)]
                        lbar[at, lane(b)] = -update if first else lbar[at, lane(b)] - update
                    cacc_s[:, lane(b)] = cacc_s[:, lane(b)] + tree(jnp.add, terms)
                return 0

            lax.fori_loop(0, rows // (8 * group), body, 0)

        @pl.when(t == 0)
        def _():
            col_pass(True)

        @pl.when(t > 0)
        def _():
            col_pass(False)

        @pl.when(t < ITERS - 1)
        def _():
            gbar_buf[k, my_cell] = jnp.sum(cacc_s[...], axis=0, keepdims=True)
            send_all("cell", n_cell, my_cell, gbar_buf, gb_send, gb_recv, k)
            wait_all("cell", n_cell, my_cell, gbar_buf, gb_send, gb_recv, k)
            total = tree(jnp.add, [gbar_buf[k, p] for p in range(n_cell)])
            gbar[...] = -(jnp.exp(g_all[k] - g_all[k + 1]) * total)

        return 0

    lax.fori_loop(0, ITERS, backward, 0)

    d_high[...], d_low[...] = split(descs[...])
    c_high[...], c_low[...] = split(cells[...].T)

    my_rows = pl.ds(pl.multiple_of(my_desc * x_block, x_block), x_block)
    my_cols = pl.ds(pl.multiple_of(my_cell * y_block, y_block), y_block)

    def y_tile(owner):
        at = pl.ds(pl.multiple_of(owner * y_block, y_block), y_block)
        high, low = split(lbar[:, at])
        return (scale * dot3(c_high[...], c_low[...], high, low)).T

    def x_tile(owner):
        at = pl.ds(pl.multiple_of(owner * x_block, x_block), x_block)
        high, low = split(lbar[at, :])
        return scale * dot3(high, low, d_high[...], d_low[...])

    def scatter_copy(axis, part, got, send_sem, recv_sem, peer, slot, off):
        return pltpu.make_async_remote_copy(
            src_ref=part.at[peer],
            dst_ref=got.at[slot],
            send_sem=send_sem.at[0, off],
            recv_sem=recv_sem.at[0, slot],
            device_id={axis: peer},
            device_id_type=MESH,
        )

    def gather_copy(axis, out, send_sem, recv_sem, peer, slot, off, size):
        at = pl.ds(pl.multiple_of(slot * size, size), size)
        return pltpu.make_async_remote_copy(
            src_ref=out.at[at],
            dst_ref=out.at[at],
            send_sem=send_sem.at[1, off],
            recv_sem=recv_sem.at[1, slot],
            device_id={axis: peer},
            device_id_type=MESH,
        )

    def send_y(off, _):
        owner = rotate(my_cell, off, n_cell)
        part_y[owner] = y_tile(owner)
        scatter_copy("cell", part_y, got_y, y_send, y_recv, owner, my_cell, off).start()
        return 0

    def send_x(off, _):
        owner = rotate(my_desc, off, n_desc)
        part_x[owner] = x_tile(owner)
        scatter_copy("desc", part_x, got_x, x_send, x_recv, owner, my_desc, off).start()
        return 0

    lax.fori_loop(1, n_cell, send_y, 0)
    lax.fori_loop(1, n_desc, send_x, 0)
    got_y[my_cell] = y_tile(my_cell)
    got_x[my_desc] = x_tile(my_desc)

    def finish_scatter(axis, count, me, part, got, send_sem, recv_sem):
        for off in range(1, count):
            peer = rotate(me, off, count)
            scatter_copy(axis, part, got, send_sem, recv_sem, peer, rotate(me, -off, count), off).wait_recv()

    def start_gather(axis, count, me, out, send_sem, recv_sem, size):
        for off in range(1, count):
            gather_copy(axis, out, send_sem, recv_sem, rotate(me, off, count), me, off, size).start()

    finish_scatter("desc", n_desc, my_desc, part_x, got_x, x_send, x_recv)
    px[my_rows, :] = tree(jnp.add, [got_x[p] for p in range(n_desc)])
    start_gather("desc", n_desc, my_desc, px, x_send, x_recv, x_block)
    finish_scatter("cell", n_cell, my_cell, part_y, got_y, y_send, y_recv)
    py[my_cols, :] = tree(jnp.add, [got_y[p] for p in range(n_cell)])
    start_gather("cell", n_cell, my_cell, py, y_send, y_recv, y_block)
    for axis, count, me, part, got, out, send_sem, recv_sem, size in (
        ("desc", n_desc, my_desc, part_x, got_x, px, x_send, x_recv, x_block),
        ("cell", n_cell, my_cell, part_y, got_y, py, y_send, y_recv, y_block),
    ):
        for off in range(1, count):
            peer = rotate(me, off, count)
            source = rotate(me, -off, count)
            gather_copy(axis, out, send_sem, recv_sem, peer, source, off, size).wait_recv()
            scatter_copy(axis, part, got, send_sem, recv_sem, peer, source, off).wait_send()
            gather_copy(axis, out, send_sem, recv_sem, peer, me, off, size).wait_send()


def run_plan(n_cell, n_desc, cells, descs, g_start, cot_f, cot_g):
    rows, width = cells.shape
    cols = descs.shape[0]
    vmem = pltpu.VMEM
    dma = pltpu.SemaphoreType.DMA
    spec = pl.BlockSpec(memory_space=pltpu.VMEM)
    return pl.pallas_call(
        functools.partial(plan_kernel, n_cell, n_desc),
        out_shape=(
            jax.ShapeDtypeStruct((rows, width), F32),
            jax.ShapeDtypeStruct((cols, width), F32),
        ),
        in_specs=[spec] * 5,
        out_specs=(spec, spec),
        scratch_shapes=[
            vmem((rows, cols), F32),
            vmem((rows, cols), F32),
            vmem((rows, cols), F32),
            vmem((rows, LANES), F32),
            vmem((rows, LANES), F32),
            vmem((rows, LANES), F32),
            vmem((8, cols), F32),
            vmem((8, cols), F32),
            vmem((8, cols), F32),
            vmem((8, cols), F32),
            vmem((ITERS, 1, rows), F32),
            vmem((ITERS + 1, 1, cols), F32),
            vmem((1, cols), F32),
            vmem((cols, width), BF16),
            vmem((cols, width), BF16),
            vmem((width, rows), BF16),
            vmem((width, rows), BF16),
            vmem((ITERS, n_desc, 2, rows), F32),
            vmem((ITERS, n_cell, 2, cols), F32),
            vmem((ITERS, n_desc, 1, rows), F32),
            vmem((ITERS, n_cell, 1, cols), F32),
            dma((ITERS, n_desc)),
            dma((ITERS, n_desc)),
            dma((ITERS, n_cell)),
            dma((ITERS, n_cell)),
            dma((ITERS, n_desc)),
            dma((ITERS, n_desc)),
            dma((ITERS, n_cell)),
            dma((ITERS, n_cell)),
            vmem((n_desc, rows // n_desc, width), F32),
            vmem((n_desc, rows // n_desc, width), F32),
            vmem((n_cell, cols // n_cell, width), F32),
            vmem((n_cell, cols // n_cell, width), F32),
            dma((2, n_desc)),
            dma((2, n_desc)),
            dma((2, n_cell)),
            dma((2, n_cell)),
        ],
        compiler_params=pltpu.CompilerParams(
            collective_id=0, has_side_effects=True, vmem_limit_bytes=60 * 1024 * 1024
        ),
        name="plan",
    )(cells, descs, g_start[None, :], cot_f[None, :], cot_g[None, :])


def solution(mesh):
    n_cell = mesh.shape["cell"]
    n_desc = mesh.shape["desc"]

    def on_device(cells, descs, g_start, cot_f, cot_g):
        return run_plan(n_cell, n_desc, cells, descs, g_start, cot_f, cot_g)

    placed = (P("cell", None), P("desc", None), P("desc"), P("cell"), P("desc"))
    return jax.shard_map(
        on_device,
        mesh=mesh,
        in_specs=placed,
        out_specs=(P("cell", None), P("desc", None)),
        check_vma=False,
    )
```

profile of v0, /device:TPU:31, one launch (start us, length us, event | category | flops | bytes accessed | tf_op | source)
XLA Modules:
  0.0 223.4 jit_solution(7090007815420700611)
XLA Ops:
  0.6 219.0 %plan.1 = (f32[1024,256]{1,0:T(8,128)}, f32[2048,256]{1,0:T(8,128)}) custom-call(f32[1024,256]{1,0:T(8,128)} %cells.1, f32[2048,256]{1,0:T(8,128)} %descs.1, f32[1,2048]{1,0:T(1,128)} %bitcast.3, f32[1,1024]{1,0:T(1,128)} %bitcast.5, f32[1,2048]{1,0:T(1,128)} %bitcast.4), custom_call_target="tpu_custom_call" | custom-call | tf_op jit(solution)/shard_map/plan/pallas_call | solution.py:322
  219.7 0.0 copy-start
  219.7 2.4 %copy.9 = f32[1024,256]{1,0:T(8,128)} copy(f32[1024,256]{1,0:T(8,128)} %get-tuple-element.4) | data formatting | bytes 2097152
  222.1 0.0 copy-done
  222.1 1.3 copy.10
Async XLA Ops:
  219.7 2.4 %copy-start = (f32[2048,256]{1,0:T(8,128)S(1)}, f32[2048,256]{1,0:T(8,128)}, u32[]{:S(2)}) copy-start(f32[2048,256]{1,0:T(8,128)} %get-tuple-element.5) | copy-start | bytes 6291460
where the time goes:
time: 224 us; the launch traced here: 223 us
  Pallas kernels  219 us (98%)
  local copies, waits for them, and re-layouts  3.73 us (2%)
    pallas_call x1, Pallas kernels, run_plan(): pl.pallas_call(functools.partial(plan_kernel, n_cell, n_desc), out_shape=...  219 us

commit v1 on v0

v1 whole, which is shorter than its diff:
```python
import functools
import math

import jax
import jax.numpy as jnp
from jax import lax
from jax.experimental import pallas as pl
from jax.experimental.pallas import tpu as pltpu
from jax.sharding import PartitionSpec as P

ITERS = 4
MESH = pl.DeviceIdType.MESH
LANES = 128
F32 = jnp.float32
BF16 = jnp.bfloat16
LOG2E = math.log2(math.e)
CHUNKS = 4
PAIRS = ((0, 0), (0, 1), (1, 0), (0, 2), (2, 0), (1, 1))


def tree(op, parts):
    parts = list(parts)
    while len(parts) > 1:
        parts = [op(parts[i], parts[i + 1]) if i + 1 < len(parts) else parts[i] for i in range(0, len(parts), 2)]
    return parts[0]


def rotate(start, offset, count):
    return lax.rem(start + offset + count, count)


def split2(value):
    high = value.astype(BF16)
    return high, (value - high.astype(F32)).astype(BF16)


def split3(value):
    high = value.astype(BF16)
    rest = value - high.astype(F32)
    mid = rest.astype(BF16)
    return high, mid, (rest - mid.astype(F32)).astype(BF16)


def mm(a, b):
    return jnp.dot(a, b, preferred_element_type=F32)


def small_copy(axis, count, me, buf, send_sem, recv_sem, index, off):
    return pltpu.make_async_remote_copy(
        src_ref=buf.at[index, me],
        dst_ref=buf.at[index, me],
        send_sem=send_sem.at[index, off],
        recv_sem=recv_sem.at[index, me],
        device_id={axis: rotate(me, off, count)},
        device_id_type=MESH,
    )


def exchange(axis, count, me, buf, send_sem, recv_sem, index):
    for off in range(1, count):
        small_copy(axis, count, me, buf, send_sem, recv_sem, index, off).start()
    for off in range(1, count):
        source = rotate(me, -off, count)
        pltpu.make_async_remote_copy(
            src_ref=buf.at[index, source],
            dst_ref=buf.at[index, source],
            send_sem=send_sem.at[index, off],
            recv_sem=recv_sem.at[index, source],
            device_id={axis: rotate(me, off, count)},
            device_id_type=MESH,
        ).wait_recv()


def drain(axis, count, me, buf, send_sem, recv_sem, indices):
    for index in range(indices):
        for off in range(1, count):
            small_copy(axis, count, me, buf, send_sem, recv_sem, index, off).wait_send()


def combine(parts):
    top = tree(jnp.maximum, parts)
    return top + jnp.log(tree(jnp.add, [jnp.exp2(part - top) for part in parts])) * LOG2E


def plan_kernel(
    n_cell, n_desc,
    cells, descs, g_first, cf, cg,
    px, py,
    plan, vcol, racc_m, racc_s, cacc_m, cacc_s, wide,
    cat_c, cat_d, s_rows, t_rows, s_cat, t_cat,
    lb_high, lb_low, d_high, d_low, c_high, c_low,
    row_buf, col_buf, row_send, row_recv, col_send, col_recv,
    part_x, got_x, x_send, x_recv, part_y, got_y, y_send, y_recv,
):
    rows, width = cells.shape
    cols = descs.shape[0]
    scale = 2.0 / math.sqrt(width)
    my_cell = lax.axis_index("cell")
    my_desc = lax.axis_index("desc")
    blocks = cols // LANES
    x_block = rows // n_desc
    group = 16
    strips = 4

    barrier = pltpu.get_barrier_semaphore()
    for off in range(1, n_desc):
        pl.semaphore_signal(barrier, inc=1, device_id={"desc": rotate(my_desc, off, n_desc)}, device_id_type=MESH)
    for off in range(1, n_cell):
        pl.semaphore_signal(barrier, inc=1, device_id={"cell": rotate(my_cell, off, n_cell)}, device_id_type=MESH)

    def lane(b):
        return slice(b * LANES, (b + 1) * LANES)

    c_parts = split3(cells[...] * (scale * LOG2E))
    d_parts = split3(descs[...])
    for n, (i, j) in enumerate(PAIRS):
        cat_c[:, n * width:(n + 1) * width] = c_parts[i]
        cat_d[:, n * width:(n + 1) * width] = d_parts[j]
    d_high[...], d_low[...] = d_parts[0], d_parts[1]
    c_high[...], c_low[...] = split2(cells[...].T)

    def multiply(i, _):
        at = pl.ds(pl.multiple_of(i * 256, 256), 256)
        plan[at, :] = lax.dot_general(cat_c[at, :], cat_d[...], (((1,), (1,)), ((), ())), preferred_element_type=F32)
        return 0

    lax.fori_loop(0, rows // 256, multiply, 0)

    g_zero = g_first[...] * LOG2E
    wide[...] = jnp.broadcast_to(g_zero, (8, cols))

    def first_row(i, _):
        for u in range(strips):
            at = pl.ds(pl.multiple_of((i * strips + u) * 8, 8), 8)
            parts = [plan[at, lane(b)] + wide[:, lane(b)] for b in range(blocks)]
            top = tree(jnp.maximum, parts)
            racc_m[at, :] = top
            racc_s[at, :] = tree(jnp.add, [jnp.exp2(part - top) for part in parts])
        return 0

    lax.fori_loop(0, rows // (8 * strips), first_row, 0)
    tops = racc_m[...].T
    top = jnp.max(tops, axis=0, keepdims=True)
    total = jnp.sum(racc_s[...].T * jnp.exp2(tops - top), axis=0, keepdims=True)
    row_buf[0, my_desc] = top + jnp.log(total) * LOG2E
    pl.semaphore_wait(barrier, n_desc + n_cell - 2)
    exchange("desc", n_desc, my_desc, row_buf, row_send, row_recv, 0)
    f_one = -combine([row_buf[0, p] for p in range(n_desc)])

    def spread_rows(vector):
        vcol[...] = jnp.broadcast_to(vector, (LANES, rows)).T

    spread_rows(f_one)
    cacc_m[...] = jnp.full((8, cols), -jnp.inf, F32)
    cacc_s[...] = jnp.zeros((8, cols), F32)

    def first_col(i, _):
        base = i * (8 * group)
        for b in range(blocks):
            ats = [pl.ds(pl.multiple_of(base + 8 * u, 8), 8) for u in range(group)]
            parts = [plan[at, lane(b)] + vcol[at, :] for at in ats]
            before = cacc_m[:, lane(b)]
            top = jnp.maximum(before, tree(jnp.maximum, parts))
            cacc_m[:, lane(b)] = top
            cacc_s[:, lane(b)] = cacc_s[:, lane(b)] * jnp.exp2(before - top) + tree(
                jnp.add, [jnp.exp2(part - top) for part in parts]
            )
        return 0

    lax.fori_loop(0, rows // (8 * group), first_col, 0)
    top = jnp.max(cacc_m[...], axis=0, keepdims=True)
    total = jnp.sum(cacc_s[...] * jnp.exp2(cacc_m[...] - top), axis=0, keepdims=True)
    col_buf[0, my_cell] = top + jnp.log(total) * LOG2E
    exchange("cell", n_cell, my_cell, col_buf, col_send, col_recv, 0)
    g_one = -combine([col_buf[0, p] for p in range(n_cell)])
    wide[...] = jnp.broadcast_to(g_one, (8, cols))
    s_rows[0:1, :] = jnp.ones((1, rows), F32)
    t_rows[ITERS:ITERS + 1, :] = jnp.exp2(g_zero - g_one)
    t_rows[ITERS + 1:ITERS + 2, :] = jnp.ones((1, cols), F32)

    def make_plan(i, _):
        for u in range(strips):
            at = pl.ds(pl.multiple_of((i * strips + u) * 8, 8), 8)
            f_here = vcol[at, :]
            terms = []
            for b in range(blocks):
                value = jnp.exp2((plan[at, lane(b)] + f_here) + wide[:, lane(b)])
                plan[at, lane(b)] = value
                terms.append(value)
            racc_s[at, :] = tree(jnp.add, terms)
        return 0

    lax.fori_loop(0, rows // (8 * strips), make_plan, 0)

    def row_product():
        weights = [wide[:, lane(b)] for b in range(blocks)]

        def body(i, _):
            for u in range(strips):
                at = pl.ds(pl.multiple_of((i * strips + u) * 8, 8), 8)
                racc_s[at, :] = tree(jnp.add, [plan[at, lane(b)] * weights[b] for b in range(blocks)])
            return 0

        lax.fori_loop(0, rows // (8 * strips), body, 0)

    def row_sum(index):
        row_buf[index, my_desc] = jnp.sum(racc_s[...].T, axis=0, keepdims=True)
        exchange("desc", n_desc, my_desc, row_buf, row_send, row_recv, index)
        return tree(jnp.add, [row_buf[index, p] for p in range(n_desc)])

    def col_sum(index):
        def body(i, totals):
            for u in range(strips):
                at = pl.ds(pl.multiple_of((i * strips + u) * 8, 8), 8)
                here = vcol[at, :]
                totals = [totals[b] + plan[at, lane(b)] * here for b in range(blocks)]
            return totals

        totals = lax.fori_loop(0, rows // (8 * strips), body, [jnp.zeros((8, LANES), F32)] * blocks)
        for b in range(blocks):
            col_buf[index, my_cell, :, lane(b)] = jnp.sum(totals[b], axis=0, keepdims=True)
        exchange("cell", n_cell, my_cell, col_buf, col_send, col_recv, index)
        return tree(jnp.add, [col_buf[index, p] for p in range(n_cell)])

    def forward(k, w_last):
        u_now = 1.0 / row_sum(k)
        s_rows[pl.ds(k, 1), :] = u_now
        spread_rows(u_now)
        w_now = 1.0 / col_sum(k)

        @pl.when(k < ITERS - 1)
        def _():
            t_rows[pl.ds(ITERS + 1 + k, 1), :] = w_now
            wide[...] = jnp.broadcast_to(w_now, (8, cols))
            row_product()

        return w_now

    w_last = lax.fori_loop(1, ITERS, forward, jnp.ones((1, cols), F32))

    def backward(t, a_now):
        k = ITERS - 1 - t
        t_rows[pl.ds(k, 1), :] = a_now
        wide[...] = jnp.broadcast_to(a_now, (8, cols))
        row_product()
        u_now = s_rows[pl.ds(k, 1), :]
        fbar = -(u_now * row_sum(ITERS + t)) + jnp.where(t == 0, cf[...], 0.0)
        b_now = u_now * fbar
        s_rows[pl.ds(ITERS + k, 1), :] = b_now

        def more(_):
            spread_rows(b_now)
            w_before = t_rows[pl.ds(ITERS + k, 1), :]
            return -(w_before * w_before * col_sum(ITERS + t))

        return lax.cond(t < ITERS - 1, more, lambda _: a_now, 0)

    lax.fori_loop(0, ITERS, backward, w_last * cg[...])

    s_parts = [part.astype(F32) for part in split3(s_rows[...])]
    t_parts = [part.astype(F32) for part in split3(t_rows[...])]
    pad = LANES - 2 * ITERS * len(PAIRS)
    s_all = jnp.concatenate([s_parts[i] for i, _ in PAIRS] + [jnp.zeros((pad, rows), F32)], axis=0)
    t_all = jnp.concatenate([t_parts[j] for _, j in PAIRS] + [jnp.zeros((pad, cols), F32)], axis=0)
    s_cat[...] = s_all.T.astype(BF16)
    t_cat[...] = t_all.astype(BF16)

    y_chunk = cols // CHUNKS
    levels = n_cell.bit_length() - 1
    orders = [list(range(levels)), list(range(1, levels)) + [0]]

    def y_plan(chunk):
        steps, start, size, place = [], chunk * y_chunk, y_chunk, 0
        for bit in orders[chunk % 2]:
            mine = lax.rem(my_cell // (1 << bit), 2)
            peer = my_cell + (1 - 2 * mine) * (1 << bit)
            size = size // 2
            sent = start + (1 - mine) * size
            start = start + mine * size
            steps.append((peer, pl.multiple_of(sent, 8), pl.multiple_of(start, 8), size, place))
            place += size
        return steps

    def y_scatter(chunk, level, step):
        peer, sent, kept, size, place = step
        return pltpu.make_async_remote_copy(
            src_ref=part_y.at[pl.ds(sent, size)],
            dst_ref=got_y.at[chunk, pl.ds(place, size)],
            send_sem=y_send.at[0, chunk, level],
            recv_sem=y_recv.at[0, chunk, level],
            device_id={"cell": peer},
            device_id_type=MESH,
        )

    def y_gather(chunk, level, step, arriving=False):
        peer, sent, kept, size, place = step
        at = pl.ds(sent if arriving else kept, size)
        return pltpu.make_async_remote_copy(
            src_ref=py.at[at],
            dst_ref=py.at[at],
            send_sem=y_send.at[1, chunk, level],
            recv_sem=y_recv.at[1, chunk, level],
            device_id={"cell": peer},
            device_id_type=MESH,
        )

    plans = [y_plan(chunk) for chunk in range(CHUNKS)]

    def y_add(chunk, level):
        peer, sent, kept, size, place = plans[chunk][level]
        y_scatter(chunk, level, plans[chunk][level]).wait_recv()
        out = part_y if level + 1 < levels else py
        out[pl.ds(kept, size), :] = part_y[pl.ds(kept, size), :] + got_y[chunk, pl.ds(place, size), :]
        if level + 1 < levels:
            y_scatter(chunk, level + 1, plans[chunk][level + 1]).start()
        else:
            y_gather(chunk, level, plans[chunk][level]).start()

    def y_spread(chunk, level):
        y_gather(chunk, level, plans[chunk][level], True).wait_recv()
        if level > 0:
            y_gather(chunk, level - 1, plans[chunk][level - 1]).start()

    for chunk in range(CHUNKS):
        def y_tile(i, _):
            at = pl.ds(pl.multiple_of(chunk * y_chunk + i * 256, 256), 256)
            high, low = split2(plan[:, at] * mm(s_cat[...], t_cat[:, at]))
            lb_high[:, at], lb_low[:, at] = high, low
            part_y[at, :] = (-scale) * (mm(c_high[...], high) + (mm(c_low[...], high) + mm(c_high[...], low))).T
            return 0

        lax.fori_loop(0, y_chunk // 256, y_tile, 0)
        y_scatter(chunk, 0, plans[chunk][0]).start()

    def x_tile(owner):
        at = pl.ds(pl.multiple_of(owner * x_block, x_block), x_block)
        high, low = lb_high[at, :], lb_low[at, :]
        return (-scale) * (mm(high, d_high[...]) + (mm(low, d_high[...]) + mm(high, d_low[...])))

    def x_scatter(off, peer, slot):
        return pltpu.make_async_remote_copy(
            src_ref=part_x.at[peer],
            dst_ref=got_x.at[slot],
            send_sem=x_send.at[0, off],
            recv_sem=x_recv.at[0, slot],
            device_id={"desc": peer},
            device_id_type=MESH,
        )

    def x_gather(off, peer, slot):
        at = pl.ds(pl.multiple_of(slot * x_block, x_block), x_block)
        return pltpu.make_async_remote_copy(
            src_ref=px.at[at],
            dst_ref=px.at[at],
            send_sem=x_send.at[1, off],
            recv_sem=x_recv.at[1, slot],
            device_id={"desc": peer},
            device_id_type=MESH,
        )

    def send_x(off, _):
        owner = rotate(my_desc, off, n_desc)
        part_x[owner] = x_tile(owner)
        x_scatter(off, owner, my_desc).start()
        return 0

    lax.fori_loop(1, n_desc, send_x, 0)
    got_x[my_desc] = x_tile(my_desc)

    for level in range(levels):
        for chunk in range(CHUNKS):
            y_add(chunk, level)
        if level == 0:
            for off in range(1, n_desc):
                x_scatter(off, rotate(my_desc, off, n_desc), rotate(my_desc, -off, n_desc)).wait_recv()
            my_rows = pl.ds(pl.multiple_of(my_desc * x_block, x_block), x_block)
            px[my_rows, :] = tree(jnp.add, [got_x[p] for p in range(n_desc)])
            for off in range(1, n_desc):
                x_gather(off, rotate(my_desc, off, n_desc), my_desc).start()
    for level in reversed(range(levels)):
        for chunk in range(CHUNKS):
            y_spread(chunk, level)

    for off in range(1, n_desc):
        peer, source = rotate(my_desc, off, n_desc), rotate(my_desc, -off, n_desc)
        x_gather(off, peer, source).wait_recv()
        x_scatter(off, peer, source).wait_send()
        x_gather(off, peer, my_desc).wait_send()
    for chunk in range(CHUNKS):
        for level in range(levels):
            y_scatter(chunk, level, plans[chunk][level]).wait_send()
            y_gather(chunk, level, plans[chunk][level]).wait_send()
    drain("desc", n_desc, my_desc, row_buf, row_send, row_recv, 2 * ITERS)
    drain("cell", n_cell, my_cell, col_buf, col_send, col_recv, 2 * ITERS - 1)


def run_plan(n_cell, n_desc, cells, descs, g_start, cot_f, cot_g):
    rows, width = cells.shape
    cols = descs.shape[0]
    vmem = pltpu.VMEM
    dma = pltpu.SemaphoreType.DMA
    spec = pl.BlockSpec(memory_space=pltpu.VMEM)
    n_row, n_col = 2 * ITERS, 2 * ITERS - 1
    levels = n_cell.bit_length() - 1
    return pl.pallas_call(
        functools.partial(plan_kernel, n_cell, n_desc),
        out_shape=(
            jax.ShapeDtypeStruct((rows, width), F32),
            jax.ShapeDtypeStruct((cols, width), F32),
        ),
        in_specs=[spec] * 5,
        out_specs=(spec, spec),
        scratch_shapes=[
            vmem((rows, cols), F32),
            vmem((rows, LANES), F32),
            vmem((rows, LANES), F32),
            vmem((rows, LANES), F32),
            vmem((8, cols), F32),
            vmem((8, cols), F32),
            vmem((8, cols), F32),
            vmem((rows, len(PAIRS) * width), BF16),
            vmem((cols, len(PAIRS) * width), BF16),
            vmem((2 * ITERS, rows), F32),
            vmem((2 * ITERS, cols), F32),
            vmem((rows, LANES), BF16),
            vmem((LANES, cols), BF16),
            vmem((rows, cols), BF16),
            vmem((rows, cols), BF16),
            vmem((cols, width), BF16),
            vmem((cols, width), BF16),
            vmem((width, rows), BF16),
            vmem((width, rows), BF16),
            vmem((n_row, n_desc, 1, rows), F32),
            vmem((n_col, n_cell, 1, cols), F32),
            dma((n_row, n_desc)),
            dma((n_row, n_desc)),
            dma((n_col, n_cell)),
            dma((n_col, n_cell)),
            vmem((n_desc, rows // n_desc, width), F32),
            vmem((n_desc, rows // n_desc, width), F32),
            dma((2, n_desc)),
            dma((2, n_desc)),
            vmem((cols, width), F32),
            vmem((CHUNKS, cols // CHUNKS, width), F32),
            dma((2, CHUNKS, levels)),
            dma((2, CHUNKS, levels)),
        ],
        compiler_params=pltpu.CompilerParams(
            collective_id=0, has_side_effects=True, vmem_limit_bytes=60 * 1024 * 1024
        ),
        name="plan",
    )(cells, descs, g_start[None, :], cot_f[None, :], cot_g[None, :])


def solution(mesh):
    n_cell = mesh.shape["cell"]
    n_desc = mesh.shape["desc"]

    def on_device(cells, descs, g_start, cot_f, cot_g):
        return run_plan(n_cell, n_desc, cells, descs, g_start, cot_f, cot_g)

    placed = (P("cell", None), P("desc", None), P("desc"), P("cell"), P("desc"))
    return jax.shard_map(
        on_device,
        mesh=mesh,
        in_specs=placed,
        out_specs=(P("cell", None), P("desc", None)),
        check_vma=False,
    )
```

time: 224 us -> 152 us (0.68)
  the two profiles are of different devices: /device:TPU:31 before, /device:TPU:0 now
where the time goes in v1:
time: 152 us
  Pallas kernels  148 us (97%)
  local copies, waits for them, and re-layouts  3.73 us (2%)
    pallas_call x1, Pallas kernels, run_plan(): pl.pallas_call(functools.partial(plan_kernel, n_cell, n_desc), out_shape=...  148 us
    unnamed x4, local copies, waits for them, and re-layouts  3.73 us

profile of v1, /device:TPU:0, one launch (start us, length us, event | category | flops | bytes accessed | tf_op | source)
XLA Modules:
  0.0 152.2 jit_solution(2267852582961294937)
XLA Ops:
  0.6 147.9 %plan.1 = (f32[1024,256]{1,0:T(8,128)}, f32[2048,256]{1,0:T(8,128)}) custom-call(f32[1024,256]{1,0:T(8,128)} %cells.1, f32[2048,256]{1,0:T(8,128)} %descs.1, f32[1,2048]{1,0:T(1,128)} %bitcast.3, f32[1,1024]{1,0:T(1,128)} %bitcast.5, f32[1,2048]{1,0:T(1,128)} %bitcast.4), custom_call_target="tpu_custom_call" | custom-call | tf_op jit(solution)/shard_map/plan/pallas_call | solution.py:405
  148.5 0.0 copy-start
  148.5 2.4 %copy.9 = f32[1024,256]{1,0:T(8,128)} copy(f32[1024,256]{1,0:T(8,128)} %get-tuple-element.4) | data formatting | bytes 2097152
  150.9 0.0 copy-done
  150.9 1.3 copy.10
Async XLA Ops:
  148.5 2.4 %copy-start = (f32[2048,256]{1,0:T(8,128)S(1)}, f32[2048,256]{1,0:T(8,128)}, u32[]{:S(2)}) copy-start(f32[2048,256]{1,0:T(8,128)} %get-tuple-element.5) | copy-start | bytes 6291460

commit v2 on v1

v2 whole, which is shorter than its diff:
```python
import functools
import math

import jax
import jax.numpy as jnp
from jax import lax
from jax.experimental import pallas as pl
from jax.experimental.pallas import tpu as pltpu
from jax.sharding import PartitionSpec as P

ITERS = 4
MESH = pl.DeviceIdType.MESH
LANES = 128
F32 = jnp.float32
BF16 = jnp.bfloat16
LOG2E = math.log2(math.e)
X_CHUNKS = 2
Y_CHUNKS = 4
PIECES = 4
PAIRS = ((0, 0), (0, 1), (1, 0), (0, 2), (2, 0), (1, 1))


def tree(op, parts):
    parts = list(parts)
    while len(parts) > 1:
        parts = [op(parts[i], parts[i + 1]) if i + 1 < len(parts) else parts[i] for i in range(0, len(parts), 2)]
    return parts[0]


def rotate(start, offset, count):
    return lax.rem(start + offset + count, count)


def split2(value):
    high = value.astype(BF16)
    return high, (value - high.astype(F32)).astype(BF16)


def split3(value):
    high = value.astype(BF16)
    rest = value - high.astype(F32)
    mid = rest.astype(BF16)
    return high, mid, (rest - mid.astype(F32)).astype(BF16)


def mm(a, b):
    return jnp.dot(a, b, preferred_element_type=F32)


def small_copy(axis, count, me, buf, send_sem, recv_sem, index, off):
    return pltpu.make_async_remote_copy(
        src_ref=buf.at[index, me],
        dst_ref=buf.at[index, me],
        send_sem=send_sem.at[index, off],
        recv_sem=recv_sem.at[index, me],
        device_id={axis: rotate(me, off, count)},
        device_id_type=MESH,
    )


def exchange(axis, count, me, buf, send_sem, recv_sem, index, between):
    for off in range(1, count):
        small_copy(axis, count, me, buf, send_sem, recv_sem, index, off).start()
    between()
    for off in range(1, count):
        source = rotate(me, -off, count)
        pltpu.make_async_remote_copy(
            src_ref=buf.at[index, source],
            dst_ref=buf.at[index, source],
            send_sem=send_sem.at[index, off],
            recv_sem=recv_sem.at[index, source],
            device_id={axis: rotate(me, off, count)},
            device_id_type=MESH,
        ).wait_recv()


def flip(index, bits):
    for bit in range(bits.bit_length()):
        if bits >> bit & 1:
            index = index + (1 - 2 * lax.rem(index // (1 << bit), 2)) * (1 << bit)
    return index


def last_hop(rel):
    return rel & -rel


def bulk_schedule(count, pieces, windows):
    top = count // 2
    limit = 3
    while True:
        came = {(p, 0): -1 for p in range(pieces)}
        plan = []
        for window in range(windows):
            left = {1 << b: limit + (window == 0) for b in range(count.bit_length() - 1)}
            sent = []
            for hop in sorted(left, reverse=True):
                for (p, rel), when in sorted(came.items(), key=lambda item: (item[1], item[0])):
                    to = rel | hop
                    if when >= window or (p, to) in came or last_hop(to) != hop or rel & hop:
                        continue
                    cost = 2 if hop == top else 1
                    if left[hop] < cost:
                        continue
                    left[hop] -= cost
                    if hop == top and top > 1:
                        left[top // 2] -= 1
                    came[p, to] = window
                    sent.append((p, to))
            plan.append(sent)
        if len(came) == pieces * count:
            return plan
        limit += 1


def drain(axis, count, me, buf, send_sem, recv_sem, indices):
    for index in range(indices):
        for off in range(1, count):
            small_copy(axis, count, me, buf, send_sem, recv_sem, index, off).wait_send()


def combine(parts):
    top = tree(jnp.maximum, parts)
    return top + jnp.log(tree(jnp.add, [jnp.exp2(part - top) for part in parts])) * LOG2E


def plan_kernel(
    n_cell, n_desc,
    cells, descs, g_first, cf, cg,
    px, py,
    plan, vcol, racc_m, racc_s, cacc_m, cacc_s, wide,
    cat_c, cat_d, s_rows, t_rows, g_row, s_cat, t_cat,
    row_buf, col_buf, row_send, row_recv, col_send, col_recv,
    part_x, got_x, x_send, x_recv,
    far_cells, far_send, far_recv, swap_send, swap_recv,
    vec_buf, vec_send, vec_recv,
    slab, g_slab, cat_t, keep_h, keep_m, sum_y, y_send, y_recv,
):
    rows, width = cells.shape
    cols = descs.shape[0]
    scale = 2.0 / math.sqrt(width)
    my_cell = lax.axis_index("cell")
    my_desc = lax.axis_index("desc")
    side = lax.rem(my_desc, 2)
    blocks = cols // LANES
    y_block = cols // n_cell
    half = rows // 2
    piece = half // PIECES
    group = 16
    strips = 4
    keep = keep_h.shape[0] == n_cell * rows

    barrier = pltpu.get_barrier_semaphore()
    for off in range(1, n_desc):
        pl.semaphore_signal(barrier, inc=1, device_id={"desc": rotate(my_desc, off, n_desc)}, device_id_type=MESH)
    for off in range(1, n_cell):
        pl.semaphore_signal(barrier, inc=1, device_id={"cell": rotate(my_cell, off, n_cell)}, device_id_type=MESH)

    def lane(b):
        return slice(b * LANES, (b + 1) * LANES)

    def fill(cat, value, which):
        parts = split3(value)
        for n, pair in enumerate(PAIRS):
            cat[:, n * width:(n + 1) * width] = parts[pair[which]]
        return parts

    def contract(a, b):
        return lax.dot_general(a, b, (((1,), (1,)), ((), ())), preferred_element_type=F32)

    fill(cat_c, cells[...] * (scale * LOG2E), 0)
    fill(cat_d, descs[...], 1)

    def multiply(i, _):
        at = pl.ds(pl.multiple_of(i * 256, 256), 256)
        plan[at, :] = contract(cat_c[at, :], cat_d[...])
        return 0

    lax.fori_loop(0, rows // 256, multiply, 0)
    g_zero = g_first[...] * LOG2E
    wide[...] = jnp.broadcast_to(g_zero, (8, cols))
    pl.semaphore_wait(barrier, n_desc + n_cell - 2)

    schedule = bulk_schedule(n_cell, PIECES, 2 * ITERS - 1)

    def far_rows(p, which):
        return pl.ds(pl.multiple_of(which * half + p * piece, piece), piece)

    def far_copy(p, rel):
        hop = last_hop(rel)
        at = far_rows(p, side)
        return pltpu.make_async_remote_copy(
            src_ref=cells.at[at] if rel == hop else far_cells.at[rel ^ hop, at],
            dst_ref=far_cells.at[rel, at],
            send_sem=far_send.at[p, rel],
            recv_sem=far_recv.at[p, rel],
            device_id={"cell": flip(my_cell, hop)},
            device_id_type=MESH,
        )

    def swap_copy(p, rel, which):
        at = far_rows(p, which)
        return pltpu.make_async_remote_copy(
            src_ref=far_cells.at[rel, at],
            dst_ref=far_cells.at[rel, at],
            send_sem=swap_send.at[p, rel],
            recv_sem=swap_recv.at[p, rel],
            device_id={"desc": flip(my_desc, 1)},
            device_id_type=MESH,
        )

    def vec_copy(v, rel):
        return pltpu.make_async_remote_copy(
            src_ref=vec_buf.at[v, 0],
            dst_ref=vec_buf.at[v, rel],
            send_sem=vec_send.at[v, rel],
            recv_sem=vec_recv.at[v, rel],
            device_id={"cell": flip(my_cell, rel)},
            device_id_type=MESH,
        )

    def send_vec(v):
        for rel in range(1, n_cell):
            vec_copy(v, rel).start()

    my_slab = pl.ds(pl.multiple_of(my_cell * y_block, y_block), y_block)

    def slab_task(rel, which):
        start = pl.multiple_of(which * half, half)
        at = pl.ds(start, half)
        source = cells[at, :] if rel == 0 else far_cells[rel, at, :]
        parts = fill(cat_t, source * (scale * LOG2E), 0)
        if keep:
            put = pl.ds(pl.multiple_of(rel * rows + start, half), half)
            keep_h[put, :], keep_m[put, :] = parts[0], parts[1]
        logits = contract(cat_d[my_slab, :], cat_t[...])
        out = pl.ds(pl.multiple_of(rel * rows + start, half), half)
        g_here = jnp.concatenate([g_slab[...]] * (half // LANES), axis=1)
        slab[:, out] = jnp.exp2((logits + vec_buf[0, rel, :, at]) + g_here)

    tasks = [(0, side), (0, 1 - side)]
    seen = {}
    swapping = []
    ready = {0}

    def run_tasks(most):
        for _ in range(min(most, len(tasks))):
            rel, which = tasks.pop(0)
            if rel not in ready:
                vec_copy(0, rel).wait_recv()
                ready.add(rel)
            slab_task(rel, which)

    def window(w):
        arrived = schedule[w - 1] if 0 < w <= len(schedule) else []
        for p, rel in arrived:
            far_copy(p, rel).wait_recv()
        for p, rel in schedule[w] if w < len(schedule) else []:
            far_copy(p, rel).start()
        for p, rel in arrived:
            swap_copy(p, rel, side).start()
            swapping.append((p, rel))
            seen[rel] = seen.get(rel, 0) + 1
            if seen[rel] == PIECES:
                tasks.append((rel, side))

    def finish_swaps():
        for p, rel in swapping:
            swap_copy(p, rel, 1 - side).wait_recv()
            seen[rel, 1] = seen.get((rel, 1), 0) + 1
            if seen[rel, 1] == PIECES:
                tasks.append((rel, 1 - side))
        swapping.clear()

    window(0)

    def first_row(i, _):
        for u in range(strips):
            at = pl.ds(pl.multiple_of((i * strips + u) * 8, 8), 8)
            parts = [plan[at, lane(b)] + wide[:, lane(b)] for b in range(blocks)]
            top = tree(jnp.maximum, parts)
            racc_m[at, :] = top
            racc_s[at, :] = tree(jnp.add, [jnp.exp2(part - top) for part in parts])
        return 0

    lax.fori_loop(0, rows // (8 * strips), first_row, 0)
    tops = racc_m[...].T
    top = jnp.max(tops, axis=0, keepdims=True)
    total = jnp.sum(racc_s[...].T * jnp.exp2(tops - top), axis=0, keepdims=True)
    row_buf[0, my_desc] = top + jnp.log(total) * LOG2E
    exchange("desc", n_desc, my_desc, row_buf, row_send, row_recv, 0, lambda: None)
    f_one = -combine([row_buf[0, p] for p in range(n_desc)])
    vec_buf[0, 0] = f_one

    def spread_rows(vector):
        vcol[...] = jnp.broadcast_to(vector, (LANES, rows)).T

    spread_rows(f_one)
    cacc_m[...] = jnp.full((8, cols), -jnp.inf, F32)
    cacc_s[...] = jnp.zeros((8, cols), F32)

    def first_col(i, _):
        base = i * (8 * group)
        for b in range(blocks):
            ats = [pl.ds(pl.multiple_of(base + 8 * u, 8), 8) for u in range(group)]
            parts = [plan[at, lane(b)] + vcol[at, :] for at in ats]
            before = cacc_m[:, lane(b)]
            top = jnp.maximum(before, tree(jnp.maximum, parts))
            cacc_m[:, lane(b)] = top
            cacc_s[:, lane(b)] = cacc_s[:, lane(b)] * jnp.exp2(before - top) + tree(
                jnp.add, [jnp.exp2(part - top) for part in parts]
            )
        return 0

    lax.fori_loop(0, rows // (8 * group), first_col, 0)
    top = jnp.max(cacc_m[...], axis=0, keepdims=True)
    total = jnp.sum(cacc_s[...] * jnp.exp2(cacc_m[...] - top), axis=0, keepdims=True)
    col_buf[0, my_cell] = top + jnp.log(total) * LOG2E

    def after_first():
        send_vec(0)
        window(1)

    exchange("cell", n_cell, my_cell, col_buf, col_send, col_recv, 0, after_first)
    g_one = -combine([col_buf[0, p] for p in range(n_cell)])
    wide[...] = jnp.broadcast_to(g_one, (8, cols))
    g_row[...] = g_one
    g_slab[...] = jnp.broadcast_to(g_row[:, my_slab], (LANES, y_block)).T
    s_rows[0:1, :] = jnp.ones((1, rows), F32)
    t_rows[ITERS:ITERS + 1, :] = jnp.exp2(g_zero - g_one)
    t_rows[ITERS + 1:ITERS + 2, :] = jnp.ones((1, cols), F32)

    def make_plan(i, _):
        for u in range(strips):
            at = pl.ds(pl.multiple_of((i * strips + u) * 8, 8), 8)
            f_here = vcol[at, :]
            terms = []
            for b in range(blocks):
                value = jnp.exp2((plan[at, lane(b)] + f_here) + wide[:, lane(b)])
                plan[at, lane(b)] = value
                terms.append(value)
            racc_s[at, :] = tree(jnp.add, terms)
        return 0

    lax.fori_loop(0, rows // (8 * strips), make_plan, 0)

    def row_product(weight):
        wide[...] = jnp.broadcast_to(weight, (8, cols))
        weights = [wide[:, lane(b)] for b in range(blocks)]

        def body(i, _):
            for u in range(strips):
                at = pl.ds(pl.multiple_of((i * strips + u) * 8, 8), 8)
                racc_s[at, :] = tree(jnp.add, [plan[at, lane(b)] * weights[b] for b in range(blocks)])
            return 0

        lax.fori_loop(0, rows // (8 * strips), body, 0)

    def row_sum(index, most):
        def between():
            finish_swaps()
            run_tasks(most)

        row_buf[index, my_desc] = jnp.sum(racc_s[...].T, axis=0, keepdims=True)
        exchange("desc", n_desc, my_desc, row_buf, row_send, row_recv, index, between)
        return tree(jnp.add, [row_buf[index, p] for p in range(n_desc)])

    def col_sum(vector, v, index, w):
        def between():
            send_vec(v)
            window(w)
            run_tasks(3)

        def body(i, totals):
            for u in range(strips):
                at = pl.ds(pl.multiple_of((i * strips + u) * 8, 8), 8)
                here = vcol[at, :]
                totals = [totals[b] + plan[at, lane(b)] * here for b in range(blocks)]
            return totals

        vec_buf[v, 0] = vector
        spread_rows(vector)
        totals = lax.fori_loop(0, rows // (8 * strips), body, [jnp.zeros((8, LANES), F32)] * blocks)
        for b in range(blocks):
            col_buf[index, my_cell, :, lane(b)] = jnp.sum(totals[b], axis=0, keepdims=True)
        exchange("cell", n_cell, my_cell, col_buf, col_send, col_recv, index, between)
        return tree(jnp.add, [col_buf[index, p] for p in range(n_cell)])

    for k in range(1, ITERS):
        u_now = 1.0 / row_sum(k, 2)
        s_rows[k:k + 1, :] = u_now
        w_now = 1.0 / col_sum(u_now, k, k, k + 1)
        if k < ITERS - 1:
            t_rows[ITERS + 1 + k:ITERS + 2 + k, :] = w_now
            row_product(w_now)

    a_now = w_now * cg[...]
    for k in reversed(range(ITERS)):
        t = ITERS - 1 - k
        t_rows[k:k + 1, :] = a_now
        row_product(a_now)
        u_now = s_rows[k:k + 1, :]
        fbar = -(u_now * row_sum(ITERS + t, 2 if k > 0 else len(tasks) + 2 * n_cell))
        if k == ITERS - 1:
            fbar = fbar + cf[...]
        b_now = u_now * fbar
        s_rows[ITERS + k:ITERS + k + 1, :] = b_now
        if k > 0:
            w_before = t_rows[ITERS + k:ITERS + k + 1, :]
            a_now = -(w_before * (w_before * col_sum(b_now, ITERS + k, ITERS + t, ITERS + 1 + t)))
        else:
            vec_buf[ITERS, 0] = b_now
            send_vec(ITERS)

    pad = LANES - 2 * ITERS * len(PAIRS)

    def stack(value, which):
        parts = [part.astype(F32) for part in split3(value)]
        return jnp.concatenate([parts[pair[which]] for pair in PAIRS] + [jnp.zeros((pad, value.shape[1]), F32)], axis=0)

    s_cat[...] = stack(s_rows[...], 0).T.astype(BF16)
    t_cat[...] = stack(t_rows[...], 1).astype(BF16)

    x_chunk = rows // X_CHUNKS
    levels = n_desc.bit_length() - 1

    def x_plan(chunk):
        steps, start, size, place = [], chunk * x_chunk, x_chunk, chunk * x_chunk
        for bit in range(levels):
            mine = lax.rem(my_desc // (1 << bit), 2)
            size = size // 2
            sent = start + (1 - mine) * size
            start = start + mine * size
            steps.append((flip(my_desc, 1 << bit), pl.multiple_of(sent, 8), pl.multiple_of(start, 8), size, place))
            place += size
        return steps

    plans = [x_plan(chunk) for chunk in range(X_CHUNKS)]

    def x_scatter(chunk, level):
        peer, sent, kept, size, place = plans[chunk][level]
        return pltpu.make_async_remote_copy(
            src_ref=part_x.at[pl.ds(sent, size)],
            dst_ref=got_x.at[pl.ds(place, size)],
            send_sem=x_send.at[0, chunk, level],
            recv_sem=x_recv.at[0, chunk, level],
            device_id={"desc": peer},
            device_id_type=MESH,
        )

    def x_gather(chunk, level, arriving=False):
        peer, sent, kept, size, place = plans[chunk][level]
        at = pl.ds(sent if arriving else kept, size)
        return pltpu.make_async_remote_copy(
            src_ref=px.at[at],
            dst_ref=px.at[at],
            send_sem=x_send.at[1, chunk, level],
            recv_sem=x_recv.at[1, chunk, level],
            device_id={"desc": peer},
            device_id_type=MESH,
        )

    def x_add(chunk, level):
        peer, sent, kept, size, place = plans[chunk][level]
        x_scatter(chunk, level).wait_recv()
        out = part_x if level + 1 < levels else px
        out[pl.ds(kept, size), :] = part_x[pl.ds(kept, size), :] + got_x[pl.ds(place, size), :]
        if level + 1 < levels:
            x_scatter(chunk, level + 1).start()
        else:
            x_gather(chunk, level).start()

    def x_spread(chunk, level):
        x_gather(chunk, level, True).wait_recv()
        if level > 0:
            x_gather(chunk, level - 1).start()

    def x_tile(at):
        high, low = split2(plan[at, :] * mm(s_cat[at, :], t_cat[...]))
        d_high, d_low = cat_d[:, :width], cat_d[:, width:2 * width]
        part_x[at, :] = (-scale) * (mm(high, d_high) + (mm(low, d_high) + mm(high, d_low)))

    for chunk in range(X_CHUNKS):
        for first in (True, False):
            peer, sent, kept, size, place = plans[chunk][0]
            x_tile(pl.ds(sent if first else kept, size))
            if first:
                x_scatter(chunk, 0).start()

    for level in range(levels):
        for chunk in range(X_CHUNKS):
            x_add(chunk, level)

    for v in range(1, 2 * ITERS):
        for rel in range(1, n_cell):
            vec_copy(v, rel).wait_recv()
    t_part = stack(t_rows[:, my_slab], 1).T.astype(BF16)
    sum_y[...] = jnp.zeros((y_block, width), F32)

    def y_step(rel, _):
        at = pl.ds(pl.multiple_of(rel * rows, rows), rows)
        s_here = jnp.concatenate(
            [jnp.ones((1, rows), F32)] + [vec_buf[v, rel] for v in range(1, 2 * ITERS)], axis=0
        )
        high, low = split2(slab[:, at] * mm(t_part, stack(s_here, 0).astype(BF16)))
        if keep:
            c_high, c_mid = keep_h[at, :], keep_m[at, :]
        else:
            c_high, c_mid = split2(far_cells[rel] * (scale * LOG2E))
        sum_y[...] = sum_y[...] + (mm(high, c_high) + (mm(low, c_high) + mm(high, c_mid)))
        return 0

    if not keep:
        far_cells[0] = cells[...]
    lax.fori_loop(0, n_cell, y_step, 0)
    py[my_slab, :] = sum_y[...] * (-1.0 / LOG2E)

    y_rows = y_block // Y_CHUNKS

    def y_copy(chunk, rel, arriving=False):
        hop = last_hop(rel)
        owner = flip(my_cell, rel if arriving else rel ^ hop)
        at = pl.ds(pl.multiple_of(owner * y_block + chunk * y_rows, y_rows), y_rows)
        return pltpu.make_async_remote_copy(
            src_ref=py.at[at],
            dst_ref=py.at[at],
            send_sem=y_send.at[chunk, rel],
            recv_sem=y_recv.at[chunk, rel],
            device_id={"cell": flip(my_cell, hop)},
            device_id_type=MESH,
        )

    def y_pass(chunk, rel):
        if rel:
            y_copy(chunk, rel, True).wait_recv()
        hop = (last_hop(rel) if rel else n_cell) // 2
        while hop:
            y_copy(chunk, rel | hop).start()
            hop //= 2

    def y_level(count):
        for chunk in range(Y_CHUNKS):
            for rel in sorted(range(n_cell), reverse=True):
                if bin(rel).count("1") == count:
                    y_pass(chunk, rel)

    y_level(0)
    for count in range(1, n_cell.bit_length()):
        y_level(count)
        if count <= levels:
            for chunk in range(X_CHUNKS):
                x_spread(chunk, levels - count)
    for count in range(n_cell.bit_length(), levels + 1):
        for chunk in range(X_CHUNKS):
            x_spread(chunk, levels - count)

    for chunk in range(X_CHUNKS):
        for level in range(levels):
            x_scatter(chunk, level).wait_send()
            x_gather(chunk, level).wait_send()
    for rel in range(1, n_cell):
        for chunk in range(Y_CHUNKS):
            y_copy(chunk, rel).wait_send()
        for p in range(PIECES):
            far_copy(p, rel).wait_send()
            swap_copy(p, rel, side).wait_send()
        for v in range(2 * ITERS):
            vec_copy(v, rel).wait_send()
    drain("desc", n_desc, my_desc, row_buf, row_send, row_recv, 2 * ITERS)
    drain("cell", n_cell, my_cell, col_buf, col_send, col_recv, 2 * ITERS - 1)


def run_plan(n_cell, n_desc, cells, descs, g_start, cot_f, cot_g):
    rows, width = cells.shape
    cols = descs.shape[0]
    vmem = pltpu.VMEM
    dma = pltpu.SemaphoreType.DMA
    spec = pl.BlockSpec(memory_space=pltpu.VMEM)
    n_row, n_col = 2 * ITERS, 2 * ITERS - 1
    x_levels = n_desc.bit_length() - 1
    n_kept = n_cell if n_cell <= 8 else 1
    return pl.pallas_call(
        functools.partial(plan_kernel, n_cell, n_desc),
        out_shape=(
            vmem((rows, width), F32),
            vmem((cols, width), F32),
        ),
        in_specs=[spec] * 5,
        out_specs=(spec, spec),
        scratch_shapes=[
            vmem((rows, cols), F32),
            vmem((rows, LANES), F32),
            vmem((rows, LANES), F32),
            vmem((rows, LANES), F32),
            vmem((8, cols), F32),
            vmem((8, cols), F32),
            vmem((8, cols), F32),
            vmem((rows, len(PAIRS) * width), BF16),
            vmem((cols, len(PAIRS) * width), BF16),
            vmem((2 * ITERS, rows), F32),
            vmem((2 * ITERS, cols), F32),
            vmem((1, cols), F32),
            vmem((rows, LANES), BF16),
            vmem((LANES, cols), BF16),
            vmem((n_row, n_desc, 1, rows), F32),
            vmem((n_col, n_cell, 1, cols), F32),
            dma((n_row, n_desc)),
            dma((n_row, n_desc)),
            dma((n_col, n_cell)),
            dma((n_col, n_cell)),
            vmem((rows, width), F32),
            vmem((rows, width), F32),
            dma((2, X_CHUNKS, x_levels)),
            dma((2, X_CHUNKS, x_levels)),
            vmem((n_cell, rows, width), F32),
            dma((PIECES, n_cell)),
            dma((PIECES, n_cell)),
            dma((PIECES, n_cell)),
            dma((PIECES, n_cell)),
            vmem((2 * ITERS, n_cell, 1, rows), F32),
            dma((2 * ITERS, n_cell)),
            dma((2 * ITERS, n_cell)),
            vmem((cols // n_cell, n_cell * rows), F32),
            vmem((cols // n_cell, LANES), F32),
            vmem((rows // 2, len(PAIRS) * width), BF16),
            vmem((n_kept * rows, width), BF16),
            vmem((n_kept * rows, width), BF16),
            vmem((cols // n_cell, width), F32),
            dma((Y_CHUNKS, n_cell)),
            dma((Y_CHUNKS, n_cell)),
        ],
        compiler_params=pltpu.CompilerParams(
            collective_id=0, has_side_effects=True, vmem_limit_bytes=60 * 1024 * 1024
        ),
        name="plan",
    )(cells, descs, g_start[None, :], cot_f[None, :], cot_g[None, :])


def solution(mesh):
    n_cell = mesh.shape["cell"]
    n_desc = mesh.shape["desc"]

    def on_device(cells, descs, g_start, cot_f, cot_g):
        return run_plan(n_cell, n_desc, cells, descs, g_start, cot_f, cot_g)

    placed = (P("cell", None), P("desc", None), P("desc"), P("cell"), P("desc"))
    return jax.shard_map(
        on_device,
        mesh=mesh,
        in_specs=placed,
        out_specs=(P("cell", None), P("desc", None)),
        check_vma=False,
    )
```

time: 152 us -> 146 us (0.961)
  Pallas kernels: 148 us -> 143 us
    pallas_call x1, Pallas kernels: 148 us -> 143 us  [run_plan(): pl.pallas_call(functools.partial(plan_kernel, n_cell, n_desc), out_shape=...]
    unnamed x4 -> x2, local copies, waits for them, and re-layouts: 3.73 us -> 2.29 us
where the time goes in v2:
time: 146 us; the launch traced here: 145 us
  Pallas kernels  143 us (98%)
  local copies, waits for them, and re-layouts  2.29 us (2%)
    pallas_call x1, Pallas kernels, run_plan(): pl.pallas_call(functools.partial(plan_kernel, n_cell, n_desc), out_shape=...  143 us

profile of v2, /device:TPU:0, one launch (start us, length us, event | category | flops | bytes accessed | tf_op | source)
XLA Modules:
  0.0 145.5 jit_solution(17770066445178600671)
XLA Ops:
  0.6 142.5 %plan.1 = (f32[1024,256]{1,0:T(8,128)S(1)}, f32[2048,256]{1,0:T(8,128)S(1)}) custom-call(f32[1024,256]{1,0:T(8,128)} %cells.1, f32[2048,256]{1,0:T(8,128)} %descs.1, f32[1,2048]{1,0:T(1,128)} %bitcast.3, f32[1,1024]{1,0:T(1,128)} %bitcast.5, f32[1,2048]{1,0:T(1,128)} %bitcast.4), custom_call_target="tpu_custom_call" | custom-call | tf_op jit(solution)/shard_map/plan/pallas_call | solution.py:582
  143.2 1.0 copy.9
  144.1 1.3 copy.10

commit v3 on v2

--- a/solution.py
+++ b/solution.py
@@ -17,6 +17,8 @@
 X_CHUNKS = 2
 Y_CHUNKS = 4
 PIECES = 4
+Y_PARTS = 2
+FIRST_EXTRA = 2
 PAIRS = ((0, 0), (0, 1), (1, 0), (0, 2), (2, 0), (1, 1))
 
 
@@ -87,12 +89,12 @@
 
 def bulk_schedule(count, pieces, windows):
     top = count // 2
-    limit = 3
+    limit = 2
     while True:
         came = {(p, 0): -1 for p in range(pieces)}
         plan = []
         for window in range(windows):
-            left = {1 << b: limit + (window == 0) for b in range(count.bit_length() - 1)}
+            left = {1 << b: limit + FIRST_EXTRA * (window == 0) for b in range(count.bit_length() - 1)}
             sent = []
             for hop in sorted(left, reverse=True):
                 for (p, rel), when in sorted(came.items(), key=lambda item: (item[1], item[0])):
@@ -171,14 +173,6 @@
     fill(cat_c, cells[...] * (scale * LOG2E), 0)
     fill(cat_d, descs[...], 1)
 
-    def multiply(i, _):
-        at = pl.ds(pl.multiple_of(i * 256, 256), 256)
-        plan[at, :] = contract(cat_c[at, :], cat_d[...])
-        return 0
-
-    lax.fori_loop(0, rows // 256, multiply, 0)
-    g_zero = g_first[...] * LOG2E
-    wide[...] = jnp.broadcast_to(g_zero, (8, cols))
     pl.semaphore_wait(barrier, n_desc + n_cell - 2)
 
     schedule = bulk_schedule(n_cell, PIECES, 2 * ITERS - 1)
@@ -273,6 +267,15 @@
         swapping.clear()
 
     window(0)
+
+    def multiply(i, _):
+        at = pl.ds(pl.multiple_of(i * 256, 256), 256)
+        plan[at, :] = contract(cat_c[at, :], cat_d[...])
+        return 0
+
+    lax.fori_loop(0, rows // 256, multiply, 0)
+    g_zero = g_first[...] * LOG2E
+    wide[...] = jnp.broadcast_to(g_zero, (8, cols))
 
     def first_row(i, _):
         for u in range(strips):
@@ -480,40 +483,12 @@
         d_high, d_low = cat_d[:, :width], cat_d[:, width:2 * width]
         part_x[at, :] = (-scale) * (mm(high, d_high) + (mm(low, d_high) + mm(high, d_low)))
 
-    for chunk in range(X_CHUNKS):
+    def x_chunk_tiles(chunk):
         for first in (True, False):
             peer, sent, kept, size, place = plans[chunk][0]
             x_tile(pl.ds(sent if first else kept, size))
             if first:
                 x_scatter(chunk, 0).start()
-
-    for level in range(levels):
-        for chunk in range(X_CHUNKS):
-            x_add(chunk, level)
-
-    for v in range(1, 2 * ITERS):
-        for rel in range(1, n_cell):
-            vec_copy(v, rel).wait_recv()
-    t_part = stack(t_rows[:, my_slab], 1).T.astype(BF16)
-    sum_y[...] = jnp.zeros((y_block, width), F32)
-
-    def y_step(rel, _):
-        at = pl.ds(pl.multiple_of(rel * rows, rows), rows)
-        s_here = jnp.concatenate(
-            [jnp.ones((1, rows), F32)] + [vec_buf[v, rel] for v in range(1, 2 * ITERS)], axis=0
-        )
-        high, low = split2(slab[:, at] * mm(t_part, stack(s_here, 0).astype(BF16)))
-        if keep:
-            c_high, c_mid = keep_h[at, :], keep_m[at, :]
-        else:
-            c_high, c_mid = split2(far_cells[rel] * (scale * LOG2E))
-        sum_y[...] = sum_y[...] + (mm(high, c_high) + (mm(low, c_high) + mm(high, c_mid)))
-        return 0
-
-    if not keep:
-        far_cells[0] = cells[...]
-    lax.fori_loop(0, n_cell, y_step, 0)
-    py[my_slab, :] = sum_y[...] * (-1.0 / LOG2E)
 
     y_rows = y_block // Y_CHUNKS
 
@@ -538,21 +513,65 @@
             y_copy(chunk, rel | hop).start()
             hop //= 2
 
-    def y_level(count):
-        for chunk in range(Y_CHUNKS):
+    def y_level(count, chunks):
+        for chunk in chunks:
             for rel in sorted(range(n_cell), reverse=True):
                 if bin(rel).count("1") == count:
                     y_pass(chunk, rel)
 
-    y_level(0)
-    for count in range(1, n_cell.bit_length()):
-        y_level(count)
-        if count <= levels:
-            for chunk in range(X_CHUNKS):
-                x_spread(chunk, levels - count)
-    for count in range(n_cell.bit_length(), levels + 1):
+    x_chunk_tiles(0)
+
+    for v in range(1, 2 * ITERS):
+        for rel in range(1, n_cell):
+            vec_copy(v, rel).wait_recv()
+    t_part = stack(t_rows[:, my_slab], 1).T.astype(BF16)
+    if not keep:
+        far_cells[0] = cells[...]
+    part = y_block // Y_PARTS
+    part_chunks = Y_CHUNKS // Y_PARTS
+
+    for h in range(Y_PARTS):
+        rows_here = slice(h * part, (h + 1) * part)
+        sum_y[rows_here, :] = jnp.zeros((part, width), F32)
+
+        def y_step(rel, _):
+            at = pl.ds(pl.multiple_of(rel * rows, rows), rows)
+            s_here = jnp.concatenate(
+                [jnp.ones((1, rows), F32)] + [vec_buf[v, rel] for v in range(1, 2 * ITERS)], axis=0
+            )
+            high, low = split2(slab[rows_here, at] * mm(t_part[rows_here], stack(s_here, 0).astype(BF16)))
+            if keep:
+                c_high, c_mid = keep_h[at, :], keep_m[at, :]
+            else:
+                c_high, c_mid = split2(far_cells[rel] * (scale * LOG2E))
+            sum_y[rows_here, :] = sum_y[rows_here, :] + (mm(high, c_high) + (mm(low, c_high) + mm(high, c_mid)))
+            return 0
+
+        lax.fori_loop(0, n_cell, y_step, 0)
+        py[pl.ds(pl.multiple_of(my_cell * y_block + h * part, part), part), :] = sum_y[rows_here, :] * (-1.0 / LOG2E)
+        y_level(0, range(h * part_chunks, (h + 1) * part_chunks))
+        if h == 0:
+            for chunk in range(1):
+                x_add(chunk, 0)
+    for chunk in range(1, X_CHUNKS):
+        x_chunk_tiles(chunk)
+
+    y_level(1, range(part_chunks))
+    for chunk in range(1, X_CHUNKS):
+        x_add(chunk, 0)
+    y_level(1, range(part_chunks, Y_CHUNKS))
+    for level in range(1, levels):
         for chunk in range(X_CHUNKS):
-            x_spread(chunk, levels - count)
+            x_add(chunk, level)
+    y_level(2, range(part_chunks))
+    for chunk in range(X_CHUNKS):
+        x_spread(chunk, levels - 1)
+    y_level(2, range(part_chunks, Y_CHUNKS))
+    for level in reversed(range(levels - 1)):
+        for chunk in range(X_CHUNKS):
+            x_spread(chunk, level)
+    for count in range(3, n_cell.bit_length()):
+        y_level(count, range(Y_CHUNKS))
 
     for chunk in range(X_CHUNKS):
         for level in range(levels):

time: 146 us -> 135 us (0.925)
  Pallas kernels: 143 us -> 132 us
    pallas_call x1, Pallas kernels: 143 us -> 132 us  [run_plan(): pl.pallas_call(functools.partial(plan_kernel, n_cell, n_desc), out_shape=...]
where the time goes in v3:
time: 135 us
  Pallas kernels  132 us (98%)
  local copies, waits for them, and re-layouts  2.29 us (2%)
    pallas_call x1, Pallas kernels, run_plan(): pl.pallas_call(functools.partial(plan_kernel, n_cell, n_desc), out_shape=...  132 us

profile of v3, /device:TPU:0, one launch (start us, length us, event | category | flops | bytes accessed | tf_op | source)
XLA Modules:
  0.0 135.0 jit_solution(4383881342729513664)
XLA Ops:
  0.6 132.1 %plan.1 = (f32[1024,256]{1,0:T(8,128)S(1)}, f32[2048,256]{1,0:T(8,128)S(1)}) custom-call(f32[1024,256]{1,0:T(8,128)} %cells.1, f32[2048,256]{1,0:T(8,128)} %descs.1, f32[1,2048]{1,0:T(1,128)} %bitcast.3, f32[1,1024]{1,0:T(1,128)} %bitcast.5, f32[1,2048]{1,0:T(1,128)} %bitcast.4), custom_call_target="tpu_custom_call" | custom-call | tf_op jit(solution)/shard_map/plan/pallas_call | solution.py:601
  132.7 1.0 copy.9
  133.7 1.3 copy.10

commit v4 on v3

--- a/solution.py
+++ b/solution.py
@@ -14,7 +14,6 @@
 F32 = jnp.float32
 BF16 = jnp.bfloat16
 LOG2E = math.log2(math.e)
-X_CHUNKS = 2
 Y_CHUNKS = 4
 PIECES = 4
 Y_PARTS = 2
@@ -130,13 +129,13 @@
     n_cell, n_desc,
     cells, descs, g_first, cf, cg,
     px, py,
-    plan, vcol, racc_m, racc_s, cacc_m, cacc_s, wide,
-    cat_c, cat_d, s_rows, t_rows, g_row, s_cat, t_cat,
+    plan, vcol, racc_s, cacc_m, cacc_s, wide,
+    cat_d, s_rows, t_rows, g_row, s_cat, t_cat, x_high, x_low,
     row_buf, col_buf, row_send, row_recv, col_send, col_recv,
     part_x, got_x, x_send, x_recv,
     far_cells, far_send, far_recv, swap_send, swap_recv,
     vec_buf, vec_send, vec_recv,
-    slab, g_slab, cat_t, keep_h, keep_m, sum_y, y_send, y_recv,
+    slab, g_slab, cat_t, keep_h, keep_m, s_all, sum_y, y_send, y_recv,
 ):
     rows, width = cells.shape
     cols = descs.shape[0]
@@ -151,6 +150,7 @@
     group = 16
     strips = 4
     keep = keep_h.shape[0] == n_cell * rows
+    x_chunks = rows // (2 * x_high.shape[1])
 
     barrier = pltpu.get_barrier_semaphore()
     for off in range(1, n_desc):
@@ -170,7 +170,6 @@
     def contract(a, b):
         return lax.dot_general(a, b, (((1,), (1,)), ((), ())), preferred_element_type=F32)
 
-    fill(cat_c, cells[...] * (scale * LOG2E), 0)
     fill(cat_d, descs[...], 1)
 
     pl.semaphore_wait(barrier, n_desc + n_cell - 2)
@@ -270,7 +269,9 @@
 
     def multiply(i, _):
         at = pl.ds(pl.multiple_of(i * 256, 256), 256)
-        plan[at, :] = contract(cat_c[at, :], cat_d[...])
+        use = cat_t.at[pl.ds(pl.multiple_of(lax.rem(i, half // 256) * 256, 256), 256)]
+        fill(use, cells[at, :] * (scale * LOG2E), 0)
+        plan[at, :] = contract(use[...], cat_d[...])
         return 0
 
     lax.fori_loop(0, rows // 256, multiply, 0)
@@ -282,12 +283,12 @@
             at = pl.ds(pl.multiple_of((i * strips + u) * 8, 8), 8)
             parts = [plan[at, lane(b)] + wide[:, lane(b)] for b in range(blocks)]
             top = tree(jnp.maximum, parts)
-            racc_m[at, :] = top
+            vcol[at, :] = top
             racc_s[at, :] = tree(jnp.add, [jnp.exp2(part - top) for part in parts])
         return 0
 
     lax.fori_loop(0, rows // (8 * strips), first_row, 0)
-    tops = racc_m[...].T
+    tops = vcol[...].T
     top = jnp.max(tops, axis=0, keepdims=True)
     total = jnp.sum(racc_s[...].T * jnp.exp2(tops - top), axis=0, keepdims=True)
     row_buf[0, my_desc] = top + jnp.log(total) * LOG2E
@@ -424,7 +425,7 @@
     s_cat[...] = stack(s_rows[...], 0).T.astype(BF16)
     t_cat[...] = stack(t_rows[...], 1).astype(BF16)
 
-    x_chunk = rows // X_CHUNKS
+    x_chunk = rows // x_chunks
     levels = n_desc.bit_length() - 1
 
     def x_plan(chunk):
@@ -438,7 +439,7 @@
             place += size
         return steps
 
-    plans = [x_plan(chunk) for chunk in range(X_CHUNKS)]
+    plans = [x_plan(chunk) for chunk in range(x_chunks)]
 
     def x_scatter(chunk, level):
         peer, sent, kept, size, place = plans[chunk][level]
@@ -478,24 +479,35 @@
         if level > 0:
             x_gather(chunk, level - 1).start()
 
-    def x_tile(at):
-        high, low = split2(plan[at, :] * mm(s_cat[at, :], t_cat[...]))
+    def x_make(at, slot):
+        x_high[slot], x_low[slot] = split2(plan[at, :] * mm(s_cat[at, :], t_cat[...]))
+
+    def x_use(at, slot):
+        high, low = x_high[slot], x_low[slot]
         d_high, d_low = cat_d[:, :width], cat_d[:, width:2 * width]
         part_x[at, :] = (-scale) * (mm(high, d_high) + (mm(low, d_high) + mm(high, d_low)))
 
     def x_chunk_tiles(chunk):
-        for first in (True, False):
-            peer, sent, kept, size, place = plans[chunk][0]
-            x_tile(pl.ds(sent if first else kept, size))
-            if first:
-                x_scatter(chunk, 0).start()
-
-    y_rows = y_block // Y_CHUNKS
+        peer, sent, kept, size, place = plans[chunk][0]
+        x_make(pl.ds(sent, size), 0)
+        x_make(pl.ds(kept, size), 1)
+        x_use(pl.ds(sent, size), 0)
+        x_scatter(chunk, 0).start()
+        x_use(pl.ds(kept, size), 1)
+
+    down = [1 << bit for bit in reversed(range(n_cell.bit_length() - 1))]
+    y_orders = [down[-1:] + down[:-1]] + [down] * (Y_CHUNKS - 1)
+    y_starts = [y_block * eighth // 8 for eighth in (0, 1, 4, 6)]
+    y_sizes = [y_block * eighth // 8 for eighth in (1, 3, 2, 2)]
+
+    def y_after(chunk, rel):
+        order = y_orders[chunk]
+        return order[max([order.index(hop) + 1 for hop in order if rel & hop], default=0):]
 
     def y_copy(chunk, rel, arriving=False):
-        hop = last_hop(rel)
+        hop = [hop for hop in y_orders[chunk] if rel & hop][-1]
         owner = flip(my_cell, rel if arriving else rel ^ hop)
-        at = pl.ds(pl.multiple_of(owner * y_block + chunk * y_rows, y_rows), y_rows)
+        at = pl.ds(pl.multiple_of(owner * y_block + y_starts[chunk], 8), y_sizes[chunk])
         return pltpu.make_async_remote_copy(
             src_ref=py.at[at],
             dst_ref=py.at[at],
@@ -508,10 +520,8 @@
     def y_pass(chunk, rel):
         if rel:
             y_copy(chunk, rel, True).wait_recv()
-        hop = (last_hop(rel) if rel else n_cell) // 2
-        while hop:
+        for hop in y_after(chunk, rel):
             y_copy(chunk, rel | hop).start()
-            hop //= 2
 
     def y_level(count, chunks):
         for chunk in chunks:
@@ -530,50 +540,65 @@
     part = y_block // Y_PARTS
     part_chunks = Y_CHUNKS // Y_PARTS
 
+    for rel in range(n_cell):
+        s_here = jnp.concatenate(
+            [jnp.ones((1, rows), F32)] + [vec_buf[v, rel] for v in range(1, 2 * ITERS)], axis=0
+        )
+        s_all[:, rel * rows:(rel + 1) * rows] = stack(s_here, 0).astype(BF16)
+
     for h in range(Y_PARTS):
         rows_here = slice(h * part, (h + 1) * part)
         sum_y[rows_here, :] = jnp.zeros((part, width), F32)
 
-        def y_step(rel, _):
+        def y_make(rel, slot):
             at = pl.ds(pl.multiple_of(rel * rows, rows), rows)
-            s_here = jnp.concatenate(
-                [jnp.ones((1, rows), F32)] + [vec_buf[v, rel] for v in range(1, 2 * ITERS)], axis=0
-            )
-            high, low = split2(slab[rows_here, at] * mm(t_part[rows_here], stack(s_here, 0).astype(BF16)))
+            high, low = split2(slab[rows_here, at] * mm(t_part[rows_here], s_all[:, at]))
+            x_high[slot, rows_here, :rows], x_low[slot, rows_here, :rows] = high, low
+
+        def y_use(rel, slot):
+            at = pl.ds(pl.multiple_of(rel * rows, rows), rows)
             if keep:
                 c_high, c_mid = keep_h[at, :], keep_m[at, :]
             else:
                 c_high, c_mid = split2(far_cells[rel] * (scale * LOG2E))
+            high, low = x_high[slot, rows_here, :rows], x_low[slot, rows_here, :rows]
             sum_y[rows_here, :] = sum_y[rows_here, :] + (mm(high, c_high) + (mm(low, c_high) + mm(high, c_mid)))
+
+        def y_step(i, _):
+            y_make(2 * i + 1, 1)
+            y_use(2 * i, 0)
+            y_make(jnp.minimum(2 * i + 2, n_cell - 1), 0)
+            y_use(2 * i + 1, 1)
             return 0
 
-        lax.fori_loop(0, n_cell, y_step, 0)
+        y_make(0, 0)
+        lax.fori_loop(0, n_cell // 2, y_step, 0)
         py[pl.ds(pl.multiple_of(my_cell * y_block + h * part, part), part), :] = sum_y[rows_here, :] * (-1.0 / LOG2E)
         y_level(0, range(h * part_chunks, (h + 1) * part_chunks))
         if h == 0:
             for chunk in range(1):
                 x_add(chunk, 0)
-    for chunk in range(1, X_CHUNKS):
+    for chunk in range(1, x_chunks):
         x_chunk_tiles(chunk)
 
     y_level(1, range(part_chunks))
-    for chunk in range(1, X_CHUNKS):
+    for chunk in range(1, x_chunks):
         x_add(chunk, 0)
     y_level(1, range(part_chunks, Y_CHUNKS))
     for level in range(1, levels):
-        for chunk in range(X_CHUNKS):
+        for chunk in range(x_chunks):
             x_add(chunk, level)
     y_level(2, range(part_chunks))
-    for chunk in range(X_CHUNKS):
+    for chunk in range(x_chunks):
         x_spread(chunk, levels - 1)
     y_level(2, range(part_chunks, Y_CHUNKS))
     for level in reversed(range(levels - 1)):
-        for chunk in range(X_CHUNKS):
+        for chunk in range(x_chunks):
             x_spread(chunk, level)
     for count in range(3, n_cell.bit_length()):
         y_level(count, range(Y_CHUNKS))
 
-    for chunk in range(X_CHUNKS):
+    for chunk in range(x_chunks):
         for level in range(levels):
             x_scatter(chunk, level).wait_send()
             x_gather(chunk, level).wait_send()
@@ -597,7 +622,7 @@
     spec = pl.BlockSpec(memory_space=pltpu.VMEM)
     n_row, n_col = 2 * ITERS, 2 * ITERS - 1
     x_levels = n_desc.bit_length() - 1
-    n_kept = n_cell if n_cell <= 8 else 1
+    kept, x_chunks = (n_cell * rows, 2) if n_cell <= 8 else (16, 4)
     return pl.pallas_call(
         functools.partial(plan_kernel, n_cell, n_desc),
         out_shape=(
@@ -610,17 +635,17 @@
             vmem((rows, cols), F32),
             vmem((rows, LANES), F32),
             vmem((rows, LANES), F32),
-            vmem((rows, LANES), F32),
             vmem((8, cols), F32),
             vmem((8, cols), F32),
             vmem((8, cols), F32),
-            vmem((rows, len(PAIRS) * width), BF16),
             vmem((cols, len(PAIRS) * width), BF16),
             vmem((2 * ITERS, rows), F32),
             vmem((2 * ITERS, cols), F32),
             vmem((1, cols), F32),
             vmem((rows, LANES), BF16),
             vmem((LANES, cols), BF16),
+            vmem((2, rows // x_chunks // 2, cols), BF16),
+            vmem((2, rows // x_chunks // 2, cols), BF16),
             vmem((n_row, n_desc, 1, rows), F32),
             vmem((n_col, n_cell, 1, cols), F32),
             dma((n_row, n_desc)),
@@ -629,8 +654,8 @@
             dma((n_col, n_cell)),
             vmem((rows, width), F32),
             vmem((rows, width), F32),
-            dma((2, X_CHUNKS, x_levels)),
-            dma((2, X_CHUNKS, x_levels)),
+            dma((2, x_chunks, x_levels)),
+            dma((2, x_chunks, x_levels)),
             vmem((n_cell, rows, width), F32),
             dma((PIECES, n_cell)),
             dma((PIECES, n_cell)),
@@ -642,8 +667,9 @@
             vmem((cols // n_cell, n_cell * rows), F32),
             vmem((cols // n_cell, LANES), F32),
             vmem((rows // 2, len(PAIRS) * width), BF16),
-            vmem((n_kept * rows, width), BF16),
-            vmem((n_kept * rows, width), BF16),
+            vmem((kept, width), BF16),
+            vmem((kept, width), BF16),
+            vmem((LANES, n_cell * rows), BF16),
             vmem((cols // n_cell, width), F32),
             dma((Y_CHUNKS, n_cell)),
             dma((Y_CHUNKS, n_cell)),

time: 135 us -> 131 us (0.970)
  Pallas kernels: 132 us -> 128 us
    pallas_call x1, Pallas kernels: 132 us -> 128 us  [run_plan(): pl.pallas_call(functools.partial(plan_kernel, n_cell, n_desc), out_shape=...]
where the time goes in v4:
time: 131 us
  Pallas kernels  128 us (98%)
  local copies, waits for them, and re-layouts  2.29 us (2%)
    pallas_call x1, Pallas kernels, run_plan(): pl.pallas_call(functools.partial(plan_kernel, n_cell, n_desc), out_shape=...  128 us

profile of v4, /device:TPU:0, one launch (start us, length us, event | category | flops | bytes accessed | tf_op | source)
XLA Modules:
  0.0 130.9 jit_solution(4092697592440703697)
XLA Ops:
  0.6 128.0 %plan.1 = (f32[1024,256]{1,0:T(8,128)S(1)}, f32[2048,256]{1,0:T(8,128)S(1)}) custom-call(f32[1024,256]{1,0:T(8,128)} %cells.1, f32[2048,256]{1,0:T(8,128)} %descs.1, f32[1,2048]{1,0:T(1,128)} %bitcast.3, f32[1,1024]{1,0:T(1,128)} %bitcast.5, f32[1,2048]{1,0:T(1,128)} %bitcast.4), custom_call_target="tpu_custom_call" | custom-call | tf_op jit(solution)/shard_map/plan/pallas_call | solution.py:626
  128.7 1.0 copy.9
  129.6 1.3 %copy.10 = f32[2048,256]{1,0:T(8,128)} copy(f32[2048,256]{1,0:T(8,128)S(1)} %get-tuple-element.3) | data formatting | bytes 4194304

commit v5 on v4

--- a/solution.py
+++ b/solution.py
@@ -17,7 +17,7 @@
 Y_CHUNKS = 4
 PIECES = 4
 Y_PARTS = 2
-FIRST_EXTRA = 2
+FIRST_EXTRA = 0
 PAIRS = ((0, 0), (0, 1), (1, 0), (0, 2), (2, 0), (1, 1))
 
 
@@ -88,7 +88,7 @@
 
 def bulk_schedule(count, pieces, windows):
     top = count // 2
-    limit = 2
+    limit = 3
     while True:
         came = {(p, 0): -1 for p in range(pieces)}
         plan = []
@@ -172,7 +172,6 @@
 
     fill(cat_d, descs[...], 1)
 
-    pl.semaphore_wait(barrier, n_desc + n_cell - 2)
 
     schedule = bulk_schedule(n_cell, PIECES, 2 * ITERS - 1)
 
@@ -265,8 +264,6 @@
                 tasks.append((rel, 1 - side))
         swapping.clear()
 
-    window(0)
-
     def multiply(i, _):
         at = pl.ds(pl.multiple_of(i * 256, 256), 256)
         use = cat_t.at[pl.ds(pl.multiple_of(lax.rem(i, half // 256) * 256, 256), 256)]
@@ -275,6 +272,8 @@
         return 0
 
     lax.fori_loop(0, rows // 256, multiply, 0)
+    pl.semaphore_wait(barrier, n_desc + n_cell - 2)
+    window(0)
     g_zero = g_first[...] * LOG2E
     wide[...] = jnp.broadcast_to(g_zero, (8, cols))
 

time: 131 us -> 130 us (level)
    pallas_call x1, Pallas kernels: 128 us -> 127 us  [run_plan(): pl.pallas_call(functools.partial(plan_kernel, n_cell, n_desc), out_shape=...]
where the time goes in v5:
time: 130 us; the launch traced here: 129 us
  Pallas kernels  127 us (98%)
  local copies, waits for them, and re-layouts  2.29 us (2%)
    pallas_call x1, Pallas kernels, run_plan(): pl.pallas_call(functools.partial(plan_kernel, n_cell, n_desc), out_shape=...  127 us

profile of v5, /device:TPU:0, one launch (start us, length us, event | category | flops | bytes accessed | tf_op | source)
XLA Modules:
  0.0 129.5 jit_solution(2196221572112655274)
XLA Ops:
  0.6 126.5 %plan.1 = (f32[1024,256]{1,0:T(8,128)S(1)}, f32[2048,256]{1,0:T(8,128)S(1)}) custom-call(f32[1024,256]{1,0:T(8,128)} %cells.1, f32[2048,256]{1,0:T(8,128)} %descs.1, f32[1,2048]{1,0:T(1,128)} %bitcast.3, f32[1,1024]{1,0:T(1,128)} %bitcast.5, f32[1,2048]{1,0:T(1,128)} %bitcast.4), custom_call_target="tpu_custom_call" | custom-call | tf_op jit(solution)/shard_map/plan/pallas_call | solution.py:625
  127.2 1.0 copy.9
  128.1 1.3 %copy.10 = f32[2048,256]{1,0:T(8,128)} copy(f32[2048,256]{1,0:T(8,128)S(1)} %get-tuple-element.3) | data formatting | bytes 4194304

commit v6 on v5

--- a/solution.py
+++ b/solution.py
@@ -60,7 +60,7 @@
 
 
 def exchange(axis, count, me, buf, send_sem, recv_sem, index, between):
-    for off in range(1, count):
+    for off in sorted(range(1, count), key=lambda steps: min(steps, count - steps)):
         small_copy(axis, count, me, buf, send_sem, recv_sem, index, off).start()
     between()
     for off in range(1, count):
@@ -212,7 +212,7 @@
         )
 
     def send_vec(v):
-        for rel in range(1, n_cell):
+        for rel in reversed(range(1, n_cell)):
             vec_copy(v, rel).start()
 
     my_slab = pl.ds(pl.multiple_of(my_cell * y_block, y_block), y_block)

time: 130 us -> 130 us (level)
  no operation moved by 1% of the time
where the time goes in v6:
time: 130 us
  Pallas kernels  127 us (98%)
  local copies, waits for them, and re-layouts  2.29 us (2%)
    pallas_call x1, Pallas kernels, run_plan(): pl.pallas_call(functools.partial(plan_kernel, n_cell, n_desc), out_shape=...  127 us

profile of v6, /device:TPU:0, one launch (start us, length us, event | category | flops | bytes accessed | tf_op | source)
XLA Modules:
  0.0 129.7 jit_solution(15311980713066613141)
XLA Ops:
  0.6 126.8 %plan.1 = (f32[1024,256]{1,0:T(8,128)S(1)}, f32[2048,256]{1,0:T(8,128)S(1)}) custom-call(f32[1024,256]{1,0:T(8,128)} %cells.1, f32[2048,256]{1,0:T(8,128)} %descs.1, f32[1,2048]{1,0:T(1,128)} %bitcast.3, f32[1,1024]{1,0:T(1,128)} %bitcast.5, f32[1,2048]{1,0:T(1,128)} %bitcast.4), custom_call_target="tpu_custom_call" | custom-call | tf_op jit(solution)/shard_map/plan/pallas_call | solution.py:625
  127.4 1.0 copy.9
  128.4 1.3 %copy.10 = f32[2048,256]{1,0:T(8,128)} copy(f32[2048,256]{1,0:T(8,128)S(1)} %get-tuple-element.3) | data formatting | bytes 4194304
